TPU v7x, 32 devices: a whole 2x2x4 slice. The times are simulated.
32 devices in a mesh: fsdp: 4 (over z), tensor: 2 (over core), pool: 4 (over y, x).
Axes of the slice: x: 2, y: 2, z: 4, core: 2. Of those that a mesh axis runs over, the one named last changes fastest.
Arguments:
- hidden: bfloat16 [8192, 5120], P(('fsdp', 'pool'), 'tensor'), may hold values from -6 to 6
- queries: bfloat16 [8192, 5120], P(('fsdp', 'pool'), 'tensor'), may hold values from -200 to 200
- cotangent: bfloat16 [8192, 5120], P(('fsdp', 'pool'), 'tensor'), may hold values from -6 to 6
- segment: int32 [16, 512], P(('fsdp', 'pool')), may hold values from 0 to 15, never falling along the last dimension, each value on 1 to 384 neighbouring positions
- clip_mask: int32 [8192], P(('fsdp', 'pool')), may hold values 0 or 1
- rewards: float32 [256], P(('fsdp', 'pool')), may hold values from 0 to 1
- seq_order: int32 [256], P(('fsdp', 'pool')), may hold values from 0 to 255, each once
- kv_weight: float32 [5120, 2, 1024], P('fsdp', None, 'tensor'), may hold values from -0.078125 to 0.078125
- moment_one: float32 [5120, 2, 1024], P('fsdp', None, 'tensor'), may hold values from -60 to 60
- moment_two: float32 [5120, 2, 1024], P('fsdp', None, 'tensor'), may hold values from 1 to 10000
- dec_hidden: bfloat16 [128, 4, 5120], P(('fsdp', 'pool')), may hold values from -6 to 6
- dec_queries: bfloat16 [128, 4, 5120], P(('fsdp', 'pool'), None, 'tensor'), may hold values from -200 to 200
- kv_cache: bfloat16 [128, 256, 2, 1024], P(('fsdp', 'pool'), None, None, 'tensor'), may hold values from -6 to 6
- cache_len: int32 [128], P(('fsdp', 'pool')), may hold values from 1 to 256
Outputs:
- new_weight: float32 [5120, 2, 1024], P('fsdp', None, 'tensor')
- new_moment_one: float32 [5120, 2, 1024], P('fsdp', None, 'tensor')
- new_moment_two: float32 [5120, 2, 1024], P('fsdp', None, 'tensor')
- dec_out: bfloat16 [128, 4, 5120], P(('fsdp', 'pool'), None, 'tensor')
Inputs may be any that keep to these rules, and one draw needn't show every extreme that they name: `segment`: each row never falls; every sequence number of a row has 1 to 384 tokens. `seq_order`: each place once.
All inputs are finite; a program needn't handle non-finite values. No bound on the sum of `clip_mask` on one device may be relied on, other than what follows from the above.
Results may differ from a plain program's by a relative error of at most 0.014.
The roundings to bfloat16 on the way count: a program that leaves them out, or rounds other values in their place, can miss the bound.
Values may be sent and summed in bfloat16 or wider, within the bound.
No kernel may reach another device: no remote copies, remote signals or barrier semaphores. Data moves between devices by JAX's collectives and lax.ppermute only.
A program may use at most 128 MiB of HBM per device.

v0:
```python
import math
import jax
import jax.numpy as jnp
from jax import lax
from jax.sharding import PartitionSpec as P

D = 5120
QH = 40
KVH = 8
HD = 128
GROUP = 16
beta_one = 0.9
beta_two = 0.999
learn_rate = 0.001
weight_decay = 0.1
adam_epsilon = 1e-08
adam_step = 10.0
variance_floor = 0.04
masked_score = -1e30


def learner_grads(keys_values, queries, cotangent, segment, coefficient):
    block_rows = queries.shape[0]
    head_size = queries.shape[3]
    score_scale = 1.0 / math.sqrt(head_size)
    key_rows = keys_values[:, 0]
    value_rows = keys_values[:, 1]
    scores = (
        jnp.einsum("thrd,uhd->hrtu", queries, key_rows, preferred_element_type=jnp.float32)
        * score_scale
    )
    places = jnp.arange(block_rows)
    allowed = (segment[:, None] == segment[None, :]) & (places[None, :] <= places[:, None])
    scores = jnp.where(allowed, scores, masked_score)
    row_max = jnp.max(scores, axis=-1, keepdims=True)
    weights = jnp.exp(scores - row_max)
    attention = weights / jnp.sum(weights, axis=-1, keepdims=True)
    attention_low = attention.astype(jnp.bfloat16)
    upstream = (coefficient[:, None, None, None] * cotangent.astype(jnp.float32)).astype(
        jnp.bfloat16
    )
    grad_prob = jnp.einsum(
        "thrd,uhd->hrtu", upstream, value_rows, preferred_element_type=jnp.float32
    )
    row_inner = jnp.sum(attention * grad_prob, axis=-1, keepdims=True)
    grad_score = (attention * (grad_prob - row_inner) * score_scale).astype(jnp.bfloat16)
    grad_values = jnp.einsum(
        "hrtu,thrd->uhd", attention_low, upstream, preferred_element_type=jnp.float32
    )
    grad_keys = jnp.einsum(
        "hrtu,thrd->uhd", grad_score, queries, preferred_element_type=jnp.float32
    )
    return jnp.stack([grad_keys, grad_values], axis=1).astype(jnp.bfloat16)


def decode_attend(queries, cache, fresh, lengths):
    head_size = queries.shape[4]
    steps_here = queries.shape[1]
    capacity = cache.shape[1]
    score_scale = 1.0 / math.sqrt(head_size)
    cached = (
        jnp.einsum("bshqd,blhd->bshql", queries, cache[:, :, 0], preferred_element_type=jnp.float32)
        * score_scale
    )
    recent = (
        jnp.einsum("bshqd,bjhd->bshqj", queries, fresh[:, :, 0], preferred_element_type=jnp.float32)
        * score_scale
    )
    live = jnp.arange(capacity)[None, :] < lengths[:, None]
    cached = jnp.where(live[:, None, None, None, :], cached, masked_score)
    before = jnp.arange(steps_here)[None, :] <= jnp.arange(steps_here)[:, None]
    recent = jnp.where(before[None, :, None, None, :], recent, masked_score)
    row_max = jnp.maximum(
        jnp.max(cached, axis=-1, keepdims=True), jnp.max(recent, axis=-1, keepdims=True)
    )
    cached_exp = jnp.exp(cached - row_max)
    recent_exp = jnp.exp(recent - row_max)
    total = jnp.sum(cached_exp, axis=-1, keepdims=True) + jnp.sum(
        recent_exp, axis=-1, keepdims=True
    )
    cached_low = (cached_exp / total).astype(jnp.bfloat16)
    recent_low = (recent_exp / total).astype(jnp.bfloat16)
    output = jnp.einsum(
        "bshql,blhd->bshqd", cached_low, cache[:, :, 1], preferred_element_type=jnp.float32
    )
    output = output + jnp.einsum(
        "bshqj,bjhd->bshqd", recent_low, fresh[:, :, 1], preferred_element_type=jnp.float32
    )
    return output.astype(jnp.bfloat16).reshape(queries.shape[0], steps_here, -1)


def body(
    hidden,
    queries,
    cotangent,
    segment,
    clip_mask,
    rewards,
    seq_order,
    kv_weight,
    moment_one,
    moment_two,
    dec_hidden,
    dec_queries,
    kv_cache,
    cache_len,
):
    block_rows = hidden.shape[0]
    kv_width = kv_weight.shape[2]
    heads_here = kv_width // HD
    head_ratio = QH // KVH
    weight_low = kv_weight.astype(jnp.bfloat16)
    weight_full = lax.all_gather(weight_low, "fsdp", axis=0, tiled=True)
    tokens_full = lax.all_gather(hidden, "tensor", axis=1, tiled=True)
    projected = jnp.dot(
        tokens_full, weight_full.reshape(D, 2 * kv_width), preferred_element_type=jnp.float32
    )
    keys_values = projected.astype(jnp.bfloat16).reshape(block_rows, 2, heads_here, HD)
    shards = lax.axis_size("fsdp") * lax.axis_size("pool")
    groups_total = rewards.shape[0] * shards // GROUP
    group_of = seq_order // GROUP
    onehot = (group_of[:, None] == jnp.arange(groups_total, dtype=jnp.int32)[None, :]).astype(
        jnp.float32
    )
    stats = jnp.stack([rewards, rewards * rewards], axis=1)
    partial_sums = jnp.sum(onehot[:, :, None] * stats[:, None, :], axis=0)
    sums = lax.psum(partial_sums, ("fsdp", "pool"))
    mean = sums[:, 0] / GROUP
    spread = sums[:, 1] / GROUP - mean * mean
    denom = jnp.sqrt(jnp.maximum(spread, variance_floor))
    advantage = (rewards - jnp.sum(onehot * mean[None, :], axis=1)) / jnp.sum(
        onehot * denom[None, :], axis=1
    )
    local_seg = segment[0]
    member = (local_seg[:, None] == jnp.arange(rewards.shape[0], dtype=jnp.int32)[None, :]).astype(
        jnp.float32
    )
    coefficient = jnp.sum(member * advantage[None, :], axis=1) * clip_mask.astype(jnp.float32)
    query_rows = queries.reshape(block_rows, heads_here, head_ratio, HD)
    cot_rows = cotangent.reshape(block_rows, heads_here, head_ratio, HD)
    grad_kv = learner_grads(keys_values, query_rows, cot_rows, local_seg, coefficient).reshape(
        block_rows, 2 * kv_width
    )
    partial_value = jnp.einsum(
        "tc,tk->ck", tokens_full, grad_kv, preferred_element_type=jnp.float32
    )
    shard_grad = lax.psum_scatter(
        partial_value.reshape(kv_weight.shape[0] * lax.axis_size("fsdp"), 2, kv_width).astype(
            jnp.bfloat16
        ),
        "fsdp",
        scatter_dimension=0,
        tiled=True,
    ).astype(jnp.float32)
    grad = lax.psum(shard_grad, "pool")
    new_moment_one = beta_one * moment_one + (1.0 - beta_one) * grad
    new_moment_two = beta_two * moment_two + (1.0 - beta_two) * grad * grad
    first_hat = new_moment_one / (1.0 - beta_one**adam_step)
    second_hat = new_moment_two / (1.0 - beta_two**adam_step)
    new_weight = kv_weight - learn_rate * (
        first_hat / (jnp.sqrt(second_hat) + adam_epsilon) + weight_decay * kv_weight
    )
    dec_rows = dec_hidden.shape[0]
    steps_here = dec_hidden.shape[1]
    capacity = kv_cache.shape[1]
    rollout_low = new_weight.astype(jnp.bfloat16)
    columns = lax.all_to_all(dec_hidden, "fsdp", split_axis=2, concat_axis=0, tiled=True)
    piece_width = columns.shape[2]
    rollout_flat = rollout_low.reshape(piece_width, 2 * kv_width)
    product = jnp.dot(
        columns.reshape(dec_rows * lax.axis_size("fsdp") * steps_here, piece_width),
        rollout_flat,
        preferred_element_type=jnp.float32,
    )
    fresh = lax.psum_scatter(
        product.reshape(dec_rows * lax.axis_size("fsdp"), steps_here, 2 * kv_width),
        "fsdp",
        scatter_dimension=0,
        tiled=True,
    )
    fresh_low = fresh.astype(jnp.bfloat16).reshape(dec_rows, steps_here, 2, heads_here, HD)
    cache = kv_cache.reshape(dec_rows, capacity, 2, heads_here, HD)
    query_dec = dec_queries.reshape(dec_rows, steps_here, heads_here, head_ratio, HD)
    dec_out = decode_attend(query_dec, cache, fresh_low, cache_len)
    return (new_weight, new_moment_one, new_moment_two, dec_out)


def solution(mesh):
    return jax.shard_map(
        body,
        mesh=mesh,
        in_specs=(
            P(("fsdp", "pool"), "tensor"),
            P(("fsdp", "pool"), "tensor"),
            P(("fsdp", "pool"), "tensor"),
            P(("fsdp", "pool"), None),
            P(("fsdp", "pool")),
            P(("fsdp", "pool")),
            P(("fsdp", "pool")),
            P("fsdp", None, "tensor"),
            P("fsdp", None, "tensor"),
            P("fsdp", None, "tensor"),
            P(("fsdp", "pool"), None, None),
            P(("fsdp", "pool"), None, "tensor"),
            P(("fsdp", "pool"), None, None, "tensor"),
            P(("fsdp", "pool")),
        ),
        out_specs=(
            P("fsdp", None, "tensor"),
            P("fsdp", None, "tensor"),
            P("fsdp", None, "tensor"),
            P(("fsdp", "pool"), None, "tensor"),
        ),
        check_vma=False,
    )
```

profile of v0, /device:TPU:0, one launch (start us, length us, event | category | flops | bytes accessed | tf_op | source)
XLA Modules:
  0.0 871.9 jit_solution(16252023753719787070)
XLA Ops:
  7.2 6.2 convert_element_type.64
  13.5 0.7 all-gather.3.cloned.1.call-update
  14.3 3.0 copy.102
  17.3 4.4 copy.99
  21.8 0.1 multiply_reduce_fusion
  21.9 45.7 %psum.14 = f32[16,2]{0,1:T(2,128)S(1)} all-reduce(f32[16,2]{0,1:T(2,128)S(1)} %multiply_reduce_fusion), channel_id=1, replica_groups=mesh['fsdp'=4,'tensor'=2,'pool'=4] {'fsdp','pool'}, use_global_device_ids=true, to_apply=%region_3.4 | all-reduce | flops 32 | bytes 256 | tf_op jit(solution)/shard_map/psum | solution.py:127
  67.6 0.2 select_reduce_fusion.2
  67.8 0.1 select_reduce_fusion
  67.9 0.2 fusion.56
  68.1 132.7 %all-gather.5.cloned.1.call-done = bf16[5120,2,512]{2,1,0:T(2,128)(2,1)} async-done(((bf16[1280,2,512]{2,1,0:T(2,128)(2,1)}), bf16[5120,2,512]{2,1,0:T(2,128)(2,1)}) %all-gather.5.cloned.1.call-update) | async-done | bytes 10485776 | tf_op jit(solution)/shard_map/all_gather | solution.py:113
  200.8 12.6 %copy.142 = bf16[640,8,2,512]{3,1,2,0:T(8,128)(2,1)} copy(bf16[640,8,2,512]{3,2,1,0:T(2,128)(2,1)} %bitcast.179) | data formatting | bytes 20971520
  213.4 2.4 all-gather.3.cloned.1.call-done
  215.8 10.6 %convolution_convert_fusion.1 = bf16[512,1024]{1,0:T(8,128)(2,1)} fusion(bf16[512,5120]{1,0:T(8,128)(2,1)} %all-gather.3.cloned.1.call-done, bf16[5120,1024]{1,0:T(8,128)(2,1)} %bitcast.180), kind=kOutput, calls=%fused_computation.33 | convolution fusion | flops 5369233408 | bytes 16777216 | tf_op jit(solution)/shard_map/dot_general | solution.py:115
  226.4 2.6 reshape.138
  229.0 1.6 fusion.75
  230.6 8.5 fusion.18
  239.0 13.0 %fusion.77 = (f32[4,5,512]{2,1,0:T(8,128)S(1)}, f32[4,5,512,512]{2,3,1,0:T(8,128)}) fusion(pred[512,512]{0,1:T(8,128)(4,1)S(1)} %fusion.56, bf16[512,4,5,128]{0,3,2,1:T(8,128)(2,1)} %bitcast.187, bf16[512,1,4,128]{3,2,1,0:T(4,128)(2,1)S(1)} %get-tuple-element.27), kind=kOutput, calls=%fused_computation.99 | convolution fusion | flops 1363149312 | bytes 24420352 | tf_op jit(solution)/shard_map/sub | solution.py:36
  252.1 8.9 %fusion.43 = bf16[512,1,4,128]{0,3,2,1:T(8,128)(2,1)S(1)} fusion(bf16[512,4,5,128]{0,3,2,1:T(8,128)(2,1)S(1)} %bitcast.184, f32[512]{0:T(512)S(1)} %convert_multiply_fusion.1, f32[4,5,512,512]{2,3,1,0:T(8,128)} %get-tuple-element.31, f32[4,5,512]{2,1,0:T(8,128)S(1)} %get-tuple-element.30), kind=kOutput, calls=%fused_computation.41 | convolution fusion | flops 1356857344 | bytes 24160256 | tf_op jit(solution)/shard_map/hrtu,thrd->uhd/dot_general | solution.py:47
  261.0 27.9 %fusion.48 = bf16[512,1,4,128]{0,3,2,1:T(8,128)(2,1)S(1)} fusion(bf16[512,4,5,128]{0,3,2,1:T(8,128)(2,1)} %bitcast.188, f32[4,512,512,5]{2,1,3,0:T(8,128)} %fusion.18, f32[4,5,512,512]{2,3,1,0:T(8,128)} %get-tuple-element.31, f32[4,5,512]{2,1,0:T(8,128)S(1)} %get-tuple-element.30), kind=kOutput, calls=%fused_computation.42 | convolution fusion | flops 1379150336 | bytes 45129728 | tf_op jit(solution)/shard_map/hrtu,thrd->uhd/dot_general | solution.py:50
  288.9 0.1 pad_maximum_fusion
  289.0 10.8 %convolution_convert_fusion = bf16[1024,5120]{1,0:T(8,128)(2,1)} fusion(bf16[512,1024]{0,1:T(8,128)(2,1)S(1)} %bitcast.190, bf16[512,5120]{1,0:T(8,128)(2,1)} %all-gather.3.cloned.1.call-done), kind=kOutput, calls=%fused_computation.18 | convolution fusion | flops 5373952000 | bytes 16777216 | tf_op jit(solution)/shard_map/tc,tk->ck/dot_general | solution.py:144
  299.8 26.0 %copy.106 = bf16[5120,2,512]{2,1,0:T(2,128)(2,1)} copy(bf16[5120,2,512]{0,2,1:T(8,128)(2,1)} %bitcast.181) | data formatting | bytes 20971520 | tf_op jit(solution)/shard_map/convert_element_type | solution.py:148
  325.9 0.6 copy-done.7
  326.5 0.6 dynamic-slice
  327.8 357.9 %all-reduce.6.cloned.1.call-done = bf16[5120,2,512]{2,1,0:T(2,128)(2,1)} async-done(((bf16[5120,2,512]{2,1,0:T(2,128)(2,1)}), bf16[5120,2,512]{2,1,0:T(2,128)(2,1)}) %all-reduce.6.cloned.1.call-update) | async-done | bytes 10485776
  685.7 6.0 dynamic-slice_convert_fusion
  691.8 5.0 copy.111
  696.7 6.9 reshape.159
  703.6 12.9 %all_to_all.15 = bf16[4,2,20480]{2,1,0:T(2,128)(2,1)S(1)} all-to-all(bf16[4,2,20480]{2,1,0:T(2,128)(2,1)S(1)} %reshape.159), channel_id=1, replica_groups=mesh['fsdp'=4,'tensor'=2,'pool'=4] {'fsdp'}, dimensions={0} | all-to-all | bytes 655360 | tf_op jit(solution)/shard_map/all_to_all | solution.py:167
  716.6 7.2 reshape.160
  723.8 6.7 copy.112
  730.6 81.1 %all-reduce.4.cloned.1.call-done = f32[1280,2,512]{2,1,0:T(2,128)} async-done(((f32[1280,2,512]{2,1,0:T(2,128)}), f32[1280,2,512]{2,1,0:T(2,128)}) %all-reduce.4.cloned.1.call-update) | async-done | bytes 5242896 | tf_op jit(solution)/shard_map/psum | solution.py:155
  811.7 22.5 %fusion.73 = (bf16[1280,2,512]{2,1,0:T(2,128)(2,1)S(1)}, f32[1280,2,512]{2,1,0:T(2,128)}, f32[1280,2,512]{2,1,0:T(2,128)}, f32[1280,2,512]{2,1,0:T(2,128)}) fusion(f32[1280,2,512]{2,1,0:T(2,128)} %param.21, f32[1280,2,512]{2,1,0:T(2,128)} %all-reduce.4.cloned.1.call-done, f32[1280,2,512]{2,1,0:T(2,128)} %param.22, f32[1280,2,512]{2,1,0:T(2,128)} %param.23), kind=kLoop, calls=%fused_computation.96 | loop fusion | flops 20971520 | bytes 39321600 | tf_op jit(solution)/shard_map/convert_element_type | solution.py:166
  834.2 0.7 copy.143
  834.9 0.5 convolution_bitcast_fusion.1
  835.4 0.1 reshape.144
  835.6 1.1 copy.113
  836.7 0.2 reshape.158
  836.9 11.1 %copy.107 = bf16[8,256,2,512]{1,3,2,0:T(8,128)(2,1)} copy(bf16[8,256,2,512]{3,2,1,0:T(2,128)(2,1)} %param.26) | data formatting | bytes 8388608 | tf_op args[12]
  848.1 2.1 fusion.78
  850.2 8.5 reduce-scatter.2.cloned.1.call-done
  858.7 0.9 convert_element_type.79
  859.7 1.3 fusion.79
  861.0 0.2 fusion.63
  861.3 0.5 fusion.57
  861.8 2.3 fusion.51
  864.1 0.4 fusion.53
  864.6 0.8 reshape.156
  (40 shorter events, 0.7 us)
Async XLA Ops:
  7.2 193.7 %all-gather.5.cloned.1.call-start = ((), (), s32[]{:S(2)}) async-start(), calls=%async_computation.3 | async-start | bytes 13107200 | tf_op jit(solution)/shard_map/all_gather | solution.py:113
  13.4 202.4 %all-gather.3.cloned.1.call-start = ((), (), s32[]{:S(2)}) async-start(), calls=%async_computation.2 | async-start | bytes 7864320 | tf_op jit(solution)/shard_map/all_gather | solution.py:114
  14.2 7.5 copy-start.4
  14.2 7.5 copy-start.6
  14.2 53.6 %copy-start.2 = (s32[1,512]{1,0:T(1,128)S(1)}, s32[1,512]{1,0:T(1,128)}, u32[]{:S(2)}) copy-start(s32[1,512]{1,0:T(1,128)} %param.17) | copy-start | bytes 6148
  14.2 53.7 %copy-start.3 = (s32[512]{0:T(512)S(1)}, s32[512]{0:T(512)}, u32[]{:S(2)}) copy-start(s32[512]{0:T(512)} %param.18) | copy-start | bytes 6148
  14.2 671.5 %all-reduce.6.cloned.1.call-start = ((), (), s32[]{:S(2)}) async-start(), calls=%async_computation.6 | async-start | bytes 20971520
  325.9 0.7 copy-start.7
  325.9 485.8 %all-reduce.4.cloned.1.call-start = ((), (), s32[]{:S(2)}) async-start(), calls=%async_computation.4 | async-start | bytes 10485760 | tf_op jit(solution)/shard_map/psum | solution.py:155
  327.8 364.0 %copy-start = (bf16[8,4,5120]{2,1,0:T(4,128)(2,1)S(1)}, bf16[8,4,5120]{2,1,0:T(4,128)(2,1)}, u32[]{:S(2)}) copy-start(bf16[8,4,5120]{2,1,0:T(4,128)(2,1)} %param.24) | copy-start | bytes 983044
  691.7 167.0 %reduce-scatter.2.cloned.1.call-start = ((), (), s32[]{:S(2)}) async-start(), calls=%async_computation.5 | async-start | bytes 655360 | tf_op jit(solution)/shard_map/reduce_scatter | solution.py:175
  834.2 2.5 copy-start.1
  835.6 12.4 %copy-start.5 = (s32[8]{0:T(128)S(1)}, s32[8]{0:T(128)}, u32[]{:S(2)}) copy-start(s32[8]{0:T(128)} %param.27) | copy-start | bytes 100
Sparse Core Ops, SparseCore 0:
  13.5 187.2 all-gather.4
  202.4 13.4 all-gather.2
  326.0 359.6 all-reduce.5
  691.8 119.8 all-reduce.3
  836.9 21.8 reduce-scatter.1
where the time goes:
time: 874 us; the launch traced here: 872 us
  waiting for transfers between devices  583 us (67%)
  local copies, waits for them, and re-layouts  91.3 us (10%)
  matrix products  86.4 us (10%)
  blocking collectives  58.7 us (7%)
  other arithmetic  37.2 us (4%)
  between operations  14.7 us (2%)
    unnamed x6, waiting for transfers between devices  359 us
    all_gather x1, waiting for transfers between devices, body(): weight_full = lax.all_gather(weight_low, 'fsdp', axis=0, tiled=True)  133 us
    psum x1, waiting for transfers between devices, body(): grad = lax.psum(shard_grad, 'pool')  81.1 us
    unnamed x27, local copies, waits for them, and re-layouts  52.8 us
    psum x1, blocking collectives, body(): sums = lax.psum(partial_sums, ('fsdp', 'pool'))  45.7 us
    dot_general x1, matrix products, learner_grads(): jnp.einsum('hrtu,thrd->uhd', grad_score, queries, preferred_element_type=...  27.9 us
    convert_element_type x1, local copies, waits for them, and re-layouts, body(): partial_value.reshape(kv_weight.shape[0] * lax.axis_size('fsdp'), 2, kv_w...  26 us
    convert_element_type x1, other arithmetic, body(): rollout_low = new_weight.astype(jnp.bfloat16)  22.5 us
  transfers between devices with their start and end apart: 5, of which 5 were waited for; matrix products, arithmetic and copies ran while one was open for 7% of the time, Pallas kernels for 0%

commit v1 on v0

--- a/solution.py
+++ b/solution.py
@@ -152,7 +152,9 @@
         scatter_dimension=0,
         tiled=True,
     ).astype(jnp.float32)
-    grad = lax.psum(shard_grad, "pool")
+    grad = shard_grad
+    for hop in (1, 2):
+        grad = grad + lax.ppermute(grad, "pool", [(dev, dev ^ hop) for dev in range(4)])
     new_moment_one = beta_one * moment_one + (1.0 - beta_one) * grad
     new_moment_two = beta_two * moment_two + (1.0 - beta_two) * grad * grad
     first_hat = new_moment_one / (1.0 - beta_one**adam_step)

time: 874 us -> 989 us (1.13)
  waiting for transfers between devices: 583 us -> 690 us
    ppermute x0 -> x2, waiting for transfers between devices: none -> 188 us  [body(): lax.ppermute(grad, 'pool', [(dev, dev ^ hop) for dev in range(4)])]
    psum x1 -> x0, waiting for transfers between devices: 81.1 us -> none  [body(): grad = lax.psum(shard_grad, 'pool')]
    unnamed x6 -> x5, waiting for transfers between devices: 359 us -> 359 us
  transfers between devices with their start and end apart: 5 -> 6, of which waited for: 5 -> 6; matrix products, arithmetic and copies ran while one was open for 7% -> 6% of each run, Pallas kernels for 0% -> 0%
where the time goes in v1:
time: 989 us; the launch traced here: 988 us
  waiting for transfers between devices  690 us (70%)
  local copies, waits for them, and re-layouts  91.1 us (9%)
  matrix products  86.4 us (9%)
  blocking collectives  57.7 us (6%)
  other arithmetic  44.7 us (5%)
  between operations  14.7 us (1%)
    unnamed x5, waiting for transfers between devices  359 us
    ppermute x2, waiting for transfers between devices, body(): lax.ppermute(grad, 'pool', [(dev, dev ^ hop) for dev in range(4)])  188 us
    all_gather x1, waiting for transfers between devices, body(): weight_full = lax.all_gather(weight_low, 'fsdp', axis=0, tiled=True)  133 us
    unnamed x27, local copies, waits for them, and re-layouts  52.7 us
    psum x1, blocking collectives, body(): sums = lax.psum(partial_sums, ('fsdp', 'pool'))  45.7 us
    dot_general x1, matrix products, learner_grads(): jnp.einsum('hrtu,thrd->uhd', grad_score, queries, preferred_element_type=...  27.9 us
    convert_element_type x1, local copies, waits for them, and re-layouts, body(): partial_value.reshape(kv_weight.shape[0] * lax.axis_size('fsdp'), 2, kv_w...  26 us
    convert_element_type x1, other arithmetic, body(): rollout_low = new_weight.astype(jnp.bfloat16)  25.1 us
  transfers between devices with their start and end apart: 6, of which 6 were waited for; matrix products, arithmetic and copies ran while one was open for 6% of the time, Pallas kernels for 0%

profile of v1, /device:TPU:0, one launch (start us, length us, event | category | flops | bytes accessed | tf_op | source)
XLA Modules:
  0.0 987.6 jit_solution(6864936206732009304)
XLA Ops:
  7.2 6.2 convert_element_type.64
  13.5 0.7 all-gather.3.cloned.1.call-update
  14.3 3.0 copy.102
  17.3 4.4 copy.99
  21.9 45.7 %psum.7 = f32[16,2]{0,1:T(2,128)S(1)} all-reduce(f32[16,2]{0,1:T(2,128)S(1)} %multiply_reduce_fusion), channel_id=1, replica_groups=mesh['fsdp'=4,'tensor'=2,'pool'=4] {'fsdp','pool'}, use_global_device_ids=true, to_apply=%region_3.4 | all-reduce | flops 32 | bytes 256 | tf_op jit(solution)/shard_map/psum | solution.py:127
  67.6 0.2 select_reduce_fusion.2
  67.9 0.2 fusion.56
  68.1 132.7 %all-gather.5.cloned.1.call-done = bf16[5120,2,512]{2,1,0:T(2,128)(2,1)} async-done(((bf16[1280,2,512]{2,1,0:T(2,128)(2,1)}), bf16[5120,2,512]{2,1,0:T(2,128)(2,1)}) %all-gather.5.cloned.1.call-update) | async-done | bytes 10485776 | tf_op jit(solution)/shard_map/all_gather | solution.py:113
  200.8 12.6 %copy.142 = bf16[640,8,2,512]{3,1,2,0:T(8,128)(2,1)} copy(bf16[640,8,2,512]{3,2,1,0:T(2,128)(2,1)} %bitcast.178) | data formatting | bytes 20971520
  213.4 2.4 all-gather.3.cloned.1.call-done
  215.8 10.6 %convolution_convert_fusion.1 = bf16[512,1024]{1,0:T(8,128)(2,1)} fusion(bf16[512,5120]{1,0:T(8,128)(2,1)} %all-gather.3.cloned.1.call-done, bf16[5120,1024]{1,0:T(8,128)(2,1)} %bitcast.179), kind=kOutput, calls=%fused_computation.33 | convolution fusion | flops 5369233408 | bytes 16777216 | tf_op jit(solution)/shard_map/dot_general | solution.py:115
  226.4 2.6 reshape.138
  229.0 1.6 fusion.76
  230.6 8.5 fusion.18
  239.0 13.0 %fusion.78 = (f32[4,5,512]{2,1,0:T(8,128)S(1)}, f32[4,5,512,512]{2,3,1,0:T(8,128)}) fusion(pred[512,512]{0,1:T(8,128)(4,1)S(1)} %fusion.56, bf16[512,4,5,128]{0,3,2,1:T(8,128)(2,1)} %bitcast.187, bf16[512,1,4,128]{3,2,1,0:T(4,128)(2,1)S(1)} %get-tuple-element.27), kind=kOutput, calls=%fused_computation.100 | convolution fusion | flops 1363149312 | bytes 24420352 | tf_op jit(solution)/shard_map/sub | solution.py:36
  252.1 8.9 fusion.43
  261.0 27.9 %fusion.48 = bf16[512,1,4,128]{0,3,2,1:T(8,128)(2,1)S(1)} fusion(bf16[512,4,5,128]{0,3,2,1:T(8,128)(2,1)} %bitcast.188, f32[4,512,512,5]{2,1,3,0:T(8,128)} %fusion.18, f32[4,5,512,512]{2,3,1,0:T(8,128)} %get-tuple-element.31, f32[4,5,512]{2,1,0:T(8,128)S(1)} %get-tuple-element.30), kind=kOutput, calls=%fused_computation.42 | convolution fusion | flops 1379150336 | bytes 45129728 | tf_op jit(solution)/shard_map/hrtu,thrd->uhd/dot_general | solution.py:50
  289.0 10.8 %convolution_convert_fusion = bf16[1024,5120]{1,0:T(8,128)(2,1)} fusion(bf16[512,1024]{0,1:T(8,128)(2,1)S(1)} %bitcast.190, bf16[512,5120]{1,0:T(8,128)(2,1)} %all-gather.3.cloned.1.call-done), kind=kOutput, calls=%fused_computation.18 | convolution fusion | flops 5373952000 | bytes 16777216 | tf_op jit(solution)/shard_map/tc,tk->ck/dot_general | solution.py:144
  299.8 26.0 %copy.106 = bf16[5120,2,512]{2,1,0:T(2,128)(2,1)} copy(bf16[5120,2,512]{0,2,1:T(8,128)(2,1)} %bitcast.180) | data formatting | bytes 20971520 | tf_op jit(solution)/shard_map/convert_element_type | solution.py:148
  325.9 0.6 copy-done.7
  326.5 0.6 dynamic-slice
  327.8 357.9 %all-reduce.3.cloned.1.call-done = bf16[5120,2,512]{2,1,0:T(2,128)(2,1)} async-done(((bf16[5120,2,512]{2,1,0:T(2,128)(2,1)}), bf16[5120,2,512]{2,1,0:T(2,128)(2,1)}) %all-reduce.3.cloned.1.call-update) | async-done | bytes 10485776
  685.7 4.2 dynamic-slice_convert_fusion
  690.0 1.5 collective-permute-start
  691.5 113.1 %collective-permute-done = f32[1280,2,512]{2,1,0:T(2,128)S(1)} collective-permute-done((f32[1280,2,512]{2,1,0:T(2,128)S(1)}, f32[1280,2,512]{2,1,0:T(2,128)S(1)}, u32[]{:S(2)}, u32[]{:S(2)}) %collective-permute-start) | collective-permute-done | bytes 5242912 | tf_op jit(solution)/shard_map/ppermute | solution.py:157
  804.6 6.6 fusion.66
  811.3 1.5 collective-permute-start.1
  812.8 5.0 copy.111
  817.7 6.9 reshape.159
  824.6 12.0 %all_to_all.15 = bf16[4,2,20480]{2,1,0:T(2,128)(2,1)S(1)} all-to-all(bf16[4,2,20480]{2,1,0:T(2,128)(2,1)S(1)} %reshape.159), channel_id=1, replica_groups=mesh['fsdp'=4,'tensor'=2,'pool'=4] {'fsdp'}, dimensions={0} | all-to-all | bytes 655360 | tf_op jit(solution)/shard_map/all_to_all | solution.py:169
  836.5 7.2 reshape.160
  843.7 6.7 copy.112
  850.5 74.9 %collective-permute-done.1 = f32[1280,2,512]{2,1,0:T(2,128)} collective-permute-done((f32[1280,2,512]{2,1,0:T(2,128)}, f32[1280,2,512]{2,1,0:T(2,128)}, u32[]{:S(2)}, u32[]{:S(2)}) %collective-permute-start.1) | collective-permute-done | bytes 5242912 | tf_op jit(solution)/shard_map/ppermute | solution.py:157
  925.4 25.1 %fusion.74 = (bf16[1280,2,512]{2,1,0:T(2,128)(2,1)S(1)}, f32[1280,2,512]{2,1,0:T(2,128)}, f32[1280,2,512]{2,1,0:T(2,128)}, f32[1280,2,512]{2,1,0:T(2,128)}) fusion(f32[1280,2,512]{2,1,0:T(2,128)} %param.21, f32[1280,2,512]{2,1,0:T(2,128)} %fusion.66, f32[1280,2,512]{2,1,0:T(2,128)} %collective-permute-done.1, f32[1280,2,512]{2,1,0:T(2,128)} %param.22, ...), kind=kLoop, calls=%fused_computation.97 | loop fusion | flops 22282240 | bytes 44564480 | tf_op jit(solution)/shard_map/convert_element_type | solution.py:168
  950.4 0.7 copy.143
  951.1 0.5 convolution_bitcast_fusion.1
  951.8 1.1 copy.113
  953.0 0.2 reshape.158
  953.2 11.1 %copy.107 = bf16[8,256,2,512]{1,3,2,0:T(8,128)(2,1)} copy(bf16[8,256,2,512]{3,2,1,0:T(2,128)(2,1)} %param.26) | data formatting | bytes 8388608 | tf_op args[12]
  964.3 2.1 fusion.79
  966.5 8.0 reduce-scatter.2.cloned.1.call-done
  974.4 0.9 convert_element_type.79
  975.4 1.3 fusion.80
  976.7 0.2 fusion.63
  977.0 0.5 fusion.57
  977.5 2.3 fusion.51
  979.8 0.4 fusion.53
  980.3 0.8 reshape.156
  (42 shorter events, 1.1 us)
Async XLA Ops:
  7.2 193.7 %all-gather.5.cloned.1.call-start = ((), (), s32[]{:S(2)}) async-start(), calls=%async_computation.3 | async-start | bytes 13107200 | tf_op jit(solution)/shard_map/all_gather | solution.py:113
  13.4 202.4 %all-gather.3.cloned.1.call-start = ((), (), s32[]{:S(2)}) async-start(), calls=%async_computation.2 | async-start | bytes 7864320 | tf_op jit(solution)/shard_map/all_gather | solution.py:114
  14.2 7.5 copy-start.4
  14.2 7.5 copy-start.6
  14.2 53.6 %copy-start.2 = (s32[1,512]{1,0:T(1,128)S(1)}, s32[1,512]{1,0:T(1,128)}, u32[]{:S(2)}) copy-start(s32[1,512]{1,0:T(1,128)} %param.17) | copy-start | bytes 6148
  14.2 53.7 %copy-start.3 = (s32[512]{0:T(512)S(1)}, s32[512]{0:T(512)}, u32[]{:S(2)}) copy-start(s32[512]{0:T(512)} %param.18) | copy-start | bytes 6148
  14.2 671.5 %all-reduce.3.cloned.1.call-start = ((), (), s32[]{:S(2)}) async-start(), calls=%async_computation.5 | async-start | bytes 20971520
  325.9 0.7 copy-start.7
  325.9 648.5 %reduce-scatter.2.cloned.1.call-start = ((), (), s32[]{:S(2)}) async-start(), calls=%async_computation.4 | async-start | bytes 655360 | tf_op jit(solution)/shard_map/reduce_scatter | solution.py:177
  690.0 122.8 %copy-start = (bf16[8,4,5120]{2,1,0:T(4,128)(2,1)S(1)}, bf16[8,4,5120]{2,1,0:T(4,128)(2,1)}, u32[]{:S(2)}) copy-start(bf16[8,4,5120]{2,1,0:T(4,128)(2,1)} %param.24) | copy-start | bytes 983044
  690.0 114.7 %collective-permute-start = (f32[1280,2,512]{2,1,0:T(2,128)S(1)}, f32[1280,2,512]{2,1,0:T(2,128)S(1)}, u32[]{:S(2)}, u32[]{:S(2)}) collective-permute-start(f32[1280,2,512]{2,1,0:T(2,128)S(1)} %dynamic-slice_convert_fusion), channel_id=1, source_target_pairs={{0,1},{1,0},{2,3},{3,2},{4,5},{5,4},{6,7},{7,6},{8,9},{9,8},{10,11... | collective-permute-start | bytes 15728648 | tf_op jit(solution)/shard_map/ppermute | solution.py:157
  811.3 114.1 %collective-permute-start.1 = (f32[1280,2,512]{2,1,0:T(2,128)}, f32[1280,2,512]{2,1,0:T(2,128)}, u32[]{:S(2)}, u32[]{:S(2)}) collective-permute-start(f32[1280,2,512]{2,1,0:T(2,128)} %fusion.66), channel_id=1, source_target_pairs={{0,2},{1,3},{2,0},{3,1},{4,6},{5,7},{6,4},{7,5},{8,10},{9,11},{10,... | collective-permute-start | bytes 15728648 | tf_op jit(solution)/shard_map/ppermute | solution.py:157
  950.4 2.5 copy-start.1
  951.8 12.4 %copy-start.5 = (s32[8]{0:T(128)S(1)}, s32[8]{0:T(128)}, u32[]{:S(2)}) copy-start(s32[8]{0:T(128)} %param.27) | copy-start | bytes 100
Sparse Core Ops, SparseCore 0:
  13.5 187.2 all-gather.4
  202.4 13.4 all-gather.2
  326.0 359.6 all-reduce.2
  953.1 21.3 reduce-scatter.1
